TPU v7x, 32 devices: a whole 2x2x4 slice. The times are simulated.
32 devices in a mesh: groups: 2 (over y), dp: 2 (over x), expert: 8 (over z, core).
Axes of the slice: x: 2, y: 2, z: 4, core: 2. Of those that a mesh axis runs over, the one named last changes fastest.
Arguments:
- tokens: bfloat16 [4096, 2048], P(('groups', 'dp', 'expert')), parts along dimension 0, may hold values from -6 to 6
- routes: int32 [4096, 4], P(('groups', 'dp', 'expert')), parts along dimension 0, may hold values from 0 to 7, all different within a row; in each aligned block of 128 rows (0 to 127, 128 to 255, ...) at most 128 rows name the same one
- w_gate: bfloat16 [16, 2048, 512], P(('groups', 'expert')), parts along dimension 0, may hold values from -0.125 to 0.125
- w_up: bfloat16 [16, 2048, 512], P(('groups', 'expert')), parts along dimension 0, may hold values from -0.125 to 0.125
Outputs:
- r_factor: float32 [16, 512, 512], P(('groups', 'expert'), 'dp'), parts along dimension 0
There are 2 independent parts, one for each index of `groups`. A program takes and returns all parts, laid end to end along the dimension named above; each array names one. Nothing has to cross between parts.
Inputs may be any that keep to these rules, and one draw needn't show every extreme that they name: `routes`: each row names 4 different experts. In each aligned block of 128 rows (the tokens of one device) no expert is named by more than 128 rows, and in some block some expert is named by exactly 128 rows.
All inputs are finite; a program needn't handle non-finite values.
Results may differ from a plain program's by a relative error of at most 0.0027.
Values may be sent and summed in bfloat16 or wider, within the bound.
No kernel may reach another device: no remote copies, remote signals or barrier semaphores. Data moves between devices by JAX's collectives and lax.ppermute only.
A program may use at most 64 MiB of HBM per device.

v0:
```python
import jax
import jax.numpy as jnp
from jax import lax
from jax.sharding import PartitionSpec as P

RIDGE = 0.05


def body(tokens, routes, w_gate, w_up):
    owners = lax.axis_size("expert")
    data_ranks = lax.axis_size("dp")
    experts = w_gate.shape[0] * owners
    factor_width = w_gate.shape[2]
    model_width = tokens.shape[1]
    tok_rows, top_count = routes.shape
    capacity = min(tok_rows, 2 * tok_rows * top_count // experts)
    assigned = routes.reshape(-1)
    onehot = (assigned[:, None] == jnp.arange(experts, dtype=jnp.int32)[None, :]).astype(jnp.int32)
    position = jnp.sum(jnp.cumsum(onehot, axis=0) * onehot, axis=1) - 1
    target = assigned * capacity + position
    anchor = jnp.arange(tok_rows * top_count, dtype=jnp.int32) // top_count
    source_row = jnp.zeros((experts * capacity,), jnp.int32).at[target].set(anchor)
    filled = jnp.zeros((experts * capacity,), jnp.int32).at[target].set(1)
    outbox = jnp.where(filled[:, None] > 0, tokens[source_row], jnp.zeros((), tokens.dtype))
    outbox = outbox.reshape(experts, capacity, model_width)
    gate_matrix = w_gate[0]
    up_matrix = w_up[0]
    arrived = lax.all_to_all(outbox, "expert", split_axis=0, concat_axis=0, tiled=True)
    flattened = arrived.reshape(-1, model_width)
    gate_proj = jnp.dot(flattened, gate_matrix, preferred_element_type=jnp.float32)
    up_proj = jnp.dot(flattened, up_matrix, preferred_element_type=jnp.float32)
    hidden = (jax.nn.silu(gate_proj) * up_proj).astype(jnp.bfloat16)
    hidden = hidden.reshape(arrived.shape[0], arrived.shape[1], factor_width)
    hidden = hidden.reshape(-1, factor_width)
    gram_local = lax.dot_general(
        hidden, hidden, (((0,), (0,)), ((), ())), preferred_element_type=jnp.float32
    )
    rows_mean = data_ranks * tok_rows * top_count
    block_rows = factor_width // data_ranks
    my_rank = lax.axis_index("dp")
    summed = lax.psum(gram_local, "dp")
    regular = summed / rows_mean + RIDGE * jnp.eye(factor_width, dtype=jnp.float32)
    factor = jnp.linalg.cholesky(regular).T
    my_rows = lax.dynamic_slice_in_dim(factor, my_rank * block_rows, block_rows, 0)
    return my_rows.reshape(1, block_rows, factor_width)


def solution(mesh):
    in_specs = (
        P(("groups", "dp", "expert"), None),
        P(("groups", "dp", "expert"), None),
        P(("groups", "expert"), None, None),
        P(("groups", "expert"), None, None),
    )
    out_specs = P(("groups", "expert"), "dp", None)
    return jax.shard_map(body, mesh=mesh, in_specs=in_specs, out_specs=out_specs, check_vma=False)
```

profile of v0, /device:TPU:0, one launch (start us, length us, event | category | flops | bytes accessed | tf_op | source)
XLA Modules:
  0.0 292.4 jit_solution(2657920740436624957)
XLA Ops:
  6.5 0.0 all-reduce.3.cloned.1.call-start
  6.5 0.9 copy.15
  7.5 0.1 eq.32
  7.6 0.1 eq.28
  7.7 0.7 broadcast_multiply_fusion
  8.4 1.1 reduce-window.6
  9.5 0.2 slice_reduce_fusion
  9.8 0.1 fusion.24
  9.9 0.1 copy.14
  10.0 0.1 mul.37
  10.1 2.4 scatter_custom_fusion.1
  12.6 2.4 scatter_custom_fusion
  15.1 9.9 %gather_fusion = bf16[1024,2048]{1,0:T(8,128)(2,1)} fusion(bf16[128,2048]{1,0:T(8,128)(2,1)} %param.4, s32[1024]{0:T(1024)S(1)} %fusion.26), kind=kCustom, calls=%fused_computation | custom fusion | bytes 8392704 | tf_op jit(solution)/shard_map/gather | solution.py:24
  25.0 2.5 broadcast_select_fusion
  27.6 100.1 %all_to_all.5 = bf16[8,128,2048]{2,1,0:T(8,128)(2,1)S(1)} all-to-all(bf16[8,128,2048]{2,1,0:T(8,128)(2,1)S(1)} %broadcast_select_fusion), channel_id=1, replica_groups=mesh['groups'=2,'dp'=2,'expert'=8] {'expert'}, dimensions={0} | all-to-all | bytes 8388608 | tf_op jit(solution)/shard_map/all_to_all | solution.py:28
  127.7 1.9 copy-done.2
  129.6 3.7 %fusion = f32[1024,512]{1,0:T(8,128)} fusion(bf16[1024,2048]{1,0:T(8,128)(2,1)S(1)} %bitcast.49, bf16[1,2048,512]{2,1,0:T(8,128)(2,1)S(1)} %copy-done), kind=kOutput, calls=%fused_computation.4 | convolution fusion | flops 2147483648 | bytes 8388608 | tf_op jit(solution)/shard_map/dot_general | solution.py:31
  133.3 12.2 %fusion.7 = f32[512,512]{0,1:T(8,128)} fusion(f32[1024,512]{1,0:T(8,128)} %fusion, bf16[1024,2048]{1,0:T(8,128)(2,1)} %bitcast.50, bf16[1,2048,512]{2,1,0:T(8,128)(2,1)} %param.6), kind=kOutput, calls=%fused_computation.14 | convolution fusion | flops 2687500288 | bytes 9437184 | tf_op jit(solution)/shard_map/dot_general | solution.py:35
  145.5 0.0 all-reduce.3.cloned.1.call-update
  145.6 39.2 %all-reduce.3.cloned.1.call-done = f32[512,512]{0,1:T(8,128)} async-done(((f32[512,512]{0,1:T(8,128)}), f32[512,512]{0,1:T(8,128)}) %all-reduce.3.cloned.1.call-update) | async-done | bytes 1048592 | tf_op jit(solution)/shard_map/psum | solution.py:41
  184.7 2.4 select_add_fusion
  187.1 2.6 copy.18
  189.7 1.5 fusion.9
  191.2 1.0 copy-done.3
  192.2 11.7 %cholesky.103 = f32[128,128]{1,0:T(8,128)S(1)} custom-call(f32[128,128]{1,0:T(8,128)S(1)} %cholesky.263), custom_call_target="Cholesky" | custom-call | tf_op jit(solution)/shard_map/jit(cholesky)/cholesky | solution.py:43
  203.9 10.0 %custom-call.27 = f32[1,128,128]{1,2,0:T(8,128)S(1)} custom-call(f32[1,128,128]{2,1,0:T(8,128)S(1)} %get-tuple-element.10), custom_call_target="InvertDiagBlocksLowerTriangular" | custom-call | tf_op jit(solution)/shard_map/jit(cholesky)/cholesky | solution.py:43
  214.0 1.2 fusion.15
  215.2 1.3 convolution_subtract_fusion
  216.5 11.7 %cholesky.215 = f32[128,128]{1,0:T(8,128)S(1)} custom-call(f32[128,128]{1,0:T(8,128)S(1)} %cholesky.267), custom_call_target="Cholesky" | custom-call | tf_op jit(solution)/shard_map/jit(cholesky)/cholesky | solution.py:43
  228.2 0.7 copy.21
  229.0 0.1 copy.20
  229.1 0.7 copy.19
  229.8 10.4 %custom-call.28 = f32[1,128,128]{1,2,0:T(8,128)} custom-call(f32[1,128,128]{2,1,0:T(8,128)S(1)} %get-tuple-element.8), custom_call_target="InvertDiagBlocksLowerTriangular" | custom-call | tf_op jit(solution)/shard_map/jit(cholesky)/cholesky | solution.py:43
  240.2 1.0 cholesky.222
  241.2 0.8 constant_dynamic-update-slice_fusion.2
  242.1 1.2 convolution_dynamic-update-slice_fusion
  243.2 1.5 convolution_subtract_fusion.1
  244.8 11.7 %cholesky.236 = f32[128,128]{1,0:T(8,128)S(1)} custom-call(f32[128,128]{1,0:T(8,128)S(1)} %cholesky.272), custom_call_target="Cholesky" | custom-call | tf_op jit(solution)/shard_map/jit(cholesky)/cholesky | solution.py:43
  256.5 0.1 copy.23
  256.6 10.0 %custom-call.29 = f32[1,128,128]{1,2,0:T(8,128)S(1)} custom-call(f32[1,128,128]{2,1,0:T(8,128)S(1)} %get-tuple-element.6), custom_call_target="InvertDiagBlocksLowerTriangular" | custom-call | tf_op jit(solution)/shard_map/jit(cholesky)/cholesky | solution.py:43
  266.6 0.3 convolution_dynamic-update-slice_fusion.1
  266.9 1.3 convolution_subtract_fusion.2
  268.3 11.7 %cholesky.253 = f32[128,128]{1,0:T(8,128)S(1)} custom-call(f32[128,128]{1,0:T(8,128)S(1)} %convolution_subtract_fusion.2), custom_call_target="Cholesky" | custom-call | tf_op jit(solution)/shard_map/jit(cholesky)/cholesky | solution.py:43
  280.0 0.1 copy.25
  280.1 0.7 compare_reduce_fusion.1
  280.8 0.6 compare_reduce_fusion
  281.5 0.7 compare_reduce_fusion.2
  284.7 0.9 fusion.12
  (25 shorter events, 0.3 us)
Async XLA Ops:
  6.5 123.1 %copy-start = (bf16[1,2048,512]{2,1,0:T(8,128)(2,1)S(1)}, bf16[1,2048,512]{2,1,0:T(8,128)(2,1)}, u32[]{:S(2)}) copy-start(bf16[1,2048,512]{2,1,0:T(8,128)(2,1)} %param.7) | copy-start | bytes 6291460
  6.5 178.2 %all-reduce.3.cloned.1.call-start = ((), (), s32[]{:S(2)}) async-start(), calls=%async_computation.1 | async-start | bytes 2097152 | tf_op jit(solution)/shard_map/psum | solution.py:41
  127.7 1.9 copy-start.2
  184.7 5.0 %copy-start.1 = (f32[512,512]{0,1:T(8,128)S(1)}, f32[512,512]{0,1:T(8,128)}, u32[]{:S(2)}) copy-start(f32[512,512]{0,1:T(8,128)} %all-reduce.3.cloned.1.call-done) | copy-start | bytes 3145732
  191.2 1.0 copy-start.3
Sparse Core Ops, SparseCore 0:
  145.7 38.9 all-reduce.2
where the time goes:
time: 293 us; the launch traced here: 292 us
  blocking collectives  100 us (34%)
  other arithmetic  88.8 us (30%)
  waiting for transfers between devices  39.2 us (13%)
  local copies, waits for them, and re-layouts  25.6 us (9%)
  matrix products  22.7 us (8%)
  between operations  16.1 us (5%)
    all_to_all x1, blocking collectives, body(): lax.all_to_all(outbox, 'expert', split_axis=0, concat_axis=0, tiled=True)  100 us
    another operation x14, other arithmetic, body(): factor = jnp.linalg.cholesky(regular).T  79.4 us
    psum x1, waiting for transfers between devices, body(): summed = lax.psum(gram_local, 'dp')  39.2 us
    dot_general x1, matrix products, body(): lax.dot_general(hidden, hidden, (((0,), (0,)), ((), ())), preferred_eleme...  12.2 us
    gather x1, local copies, waits for them, and re-layouts, body(): tokens[source_row]  9.94 us
    another operation x6, matrix products, body(): factor = jnp.linalg.cholesky(regular).T  6.75 us
  transfers between devices with their start and end apart: 1, of which 1 were waited for; matrix products, arithmetic and copies ran while one was open for 0% of the time, Pallas kernels for 0%

commit v1 on v0

--- a/solution.py
+++ b/solution.py
@@ -38,7 +38,8 @@
     rows_mean = data_ranks * tok_rows * top_count
     block_rows = factor_width // data_ranks
     my_rank = lax.axis_index("dp")
-    summed = lax.psum(gram_local, "dp")
+    parts = lax.all_gather(gram_local, "dp")
+    summed = jnp.sum(parts, axis=0)
     regular = summed / rows_mean + RIDGE * jnp.eye(factor_width, dtype=jnp.float32)
     factor = jnp.linalg.cholesky(regular).T
     my_rows = lax.dynamic_slice_in_dim(factor, my_rank * block_rows, block_rows, 0)

time: 293 us -> 283 us (0.966)
  waiting for transfers between devices: 39.2 us -> 32.2 us
    psum x1 -> x0, waiting for transfers between devices: 39.2 us -> none  [body(): summed = lax.psum(gram_local, 'dp')]
    all_gather x0 -> x1, waiting for transfers between devices: none -> 32.2 us  [body(): parts = lax.all_gather(gram_local, 'dp')]
    another operation x13 -> x4, local copies, waits for them, and re-layouts: 3.62 us -> 0.14 us  [body(): factor = jnp.linalg.cholesky(regular).T]
where the time goes in v1:
time: 283 us
  blocking collectives  100 us (35%)
  other arithmetic  88.7 us (31%)
  waiting for transfers between devices  32.2 us (11%)
  local copies, waits for them, and re-layouts  24.1 us (9%)
  matrix products  21.4 us (8%)
  between operations  16.2 us (6%)
    all_to_all x1, blocking collectives, body(): lax.all_to_all(outbox, 'expert', split_axis=0, concat_axis=0, tiled=True)  100 us
    another operation x14, other arithmetic, body(): factor = jnp.linalg.cholesky(regular).T  78.9 us
    all_gather x1, waiting for transfers between devices, body(): parts = lax.all_gather(gram_local, 'dp')  32.2 us
    dot_general x1, matrix products, body(): lax.dot_general(hidden, hidden, (((0,), (0,)), ((), ())), preferred_eleme...  12.2 us
    gather x1, local copies, waits for them, and re-layouts, body(): tokens[source_row]  9.94 us
  transfers between devices with their start and end apart: 1, of which 1 were waited for; matrix products, arithmetic and copies ran while one was open for 0% of the time, Pallas kernels for 0%

profile of v1, /device:TPU:0, one launch (start us, length us, event | category | flops | bytes accessed | tf_op | source)
XLA Modules:
  0.0 282.7 jit_solution(14788520626387545739)
XLA Ops:
  6.5 0.0 copy-start
  6.5 0.0 all-gather.3.cloned.1.call-start
  6.5 0.9 copy.8
  7.5 0.1 eq.35
  7.6 0.1 eq.31
  7.7 0.7 broadcast_multiply_fusion
  8.4 1.1 reduce-window.6
  9.5 0.2 slice_reduce_fusion
  9.8 0.1 fusion.23
  9.9 0.1 copy.7
  10.0 0.1 mul.39
  10.1 2.4 scatter_custom_fusion.1
  12.6 2.4 scatter_custom_fusion
  15.1 9.9 %gather_fusion = bf16[1024,2048]{1,0:T(8,128)(2,1)} fusion(bf16[128,2048]{1,0:T(8,128)(2,1)} %param.4, s32[1024]{0:T(1024)S(1)} %fusion.25), kind=kCustom, calls=%fused_computation | custom fusion | bytes 8392704 | tf_op jit(solution)/shard_map/gather | solution.py:24
  25.0 2.5 broadcast_select_fusion
  27.6 100.1 %all_to_all.5 = bf16[8,128,2048]{2,1,0:T(8,128)(2,1)S(1)} all-to-all(bf16[8,128,2048]{2,1,0:T(8,128)(2,1)S(1)} %broadcast_select_fusion), channel_id=1, replica_groups=mesh['groups'=2,'dp'=2,'expert'=8] {'expert'}, dimensions={0} | all-to-all | bytes 8388608 | tf_op jit(solution)/shard_map/all_to_all | solution.py:28
  127.7 0.0 copy-start.1
  127.7 1.9 copy-done.1
  129.6 0.0 copy-done
  129.6 3.7 %fusion = f32[1024,512]{1,0:T(8,128)} fusion(bf16[1024,2048]{1,0:T(8,128)(2,1)S(1)} %bitcast.50, bf16[1,2048,512]{2,1,0:T(8,128)(2,1)S(1)} %copy-done), kind=kOutput, calls=%fused_computation.4 | convolution fusion | flops 2147483648 | bytes 8388608 | tf_op jit(solution)/shard_map/dot_general | solution.py:31
  133.3 12.2 %fusion.7 = f32[512,512]{1,0:T(8,128)} fusion(f32[1024,512]{1,0:T(8,128)} %fusion, bf16[1024,2048]{1,0:T(8,128)(2,1)} %bitcast.51, bf16[1,2048,512]{2,1,0:T(8,128)(2,1)} %param.6), kind=kOutput, calls=%fused_computation.14 | convolution fusion | flops 2687500288 | bytes 9437184 | tf_op jit(solution)/shard_map/dot_general | solution.py:35
  145.5 0.0 all-gather.3.cloned.1.call-update
  145.6 32.2 %all-gather.3.cloned.1.call-done = f32[1024,512]{1,0:T(8,128)} async-done(((f32[512,512]{1,0:T(8,128)}), f32[1024,512]{1,0:T(8,128)}) %all-gather.3.cloned.1.call-update) | async-done | bytes 2097168 | tf_op jit(solution)/shard_map/all_gather | solution.py:41
  177.7 1.9 reduce_sum.19
  179.6 1.1 multiply_bitcast_fusion
  180.7 2.6 copy.10
  183.3 1.5 add_multiply_fusion
  184.8 0.0 copy-start.2
  184.8 1.0 copy-done.2
  185.8 11.7 %cholesky.103 = f32[128,128]{1,0:T(8,128)S(1)} custom-call(f32[128,128]{1,0:T(8,128)S(1)} %cholesky.263), custom_call_target="Cholesky" | custom-call | tf_op jit(solution)/shard_map/jit(cholesky)/cholesky | solution.py:44
  197.5 0.1 cholesky.222
  197.6 10.0 %custom-call.27 = f32[1,128,128]{1,2,0:T(8,128)S(1)} custom-call(f32[1,128,128]{2,1,0:T(8,128)S(1)} %get-tuple-element.14), custom_call_target="InvertDiagBlocksLowerTriangular" | custom-call | tf_op jit(solution)/shard_map/jit(cholesky)/cholesky | solution.py:44
  207.7 1.2 constant_dynamic-update-slice_fusion.3
  208.9 1.3 convolution_subtract_fusion
  210.2 11.7 %cholesky.215 = f32[128,128]{1,0:T(8,128)S(1)} custom-call(f32[128,128]{1,0:T(8,128)S(1)} %cholesky.267), custom_call_target="Cholesky" | custom-call | tf_op jit(solution)/shard_map/jit(cholesky)/cholesky | solution.py:44
  221.9 9.8 %custom-call.28 = f32[1,128,128]{1,2,0:T(8,128)S(1)} custom-call(f32[1,128,128]{2,1,0:T(8,128)S(1)} %get-tuple-element.11), custom_call_target="InvertDiagBlocksLowerTriangular" | custom-call | tf_op jit(solution)/shard_map/jit(cholesky)/cholesky | solution.py:44
  231.7 0.3 convolution_dynamic-update-slice_fusion
  232.0 1.3 convolution_subtract_fusion.1
  233.3 11.7 %cholesky.236 = f32[128,128]{1,0:T(8,128)S(1)} custom-call(f32[128,128]{1,0:T(8,128)S(1)} %cholesky.272), custom_call_target="Cholesky" | custom-call | tf_op jit(solution)/shard_map/jit(cholesky)/cholesky | solution.py:44
  245.1 0.7 compare_reduce_fusion.1
  245.8 10.0 %custom-call.29 = f32[1,128,128]{1,2,0:T(8,128)S(1)} custom-call(f32[1,128,128]{2,1,0:T(8,128)S(1)} %get-tuple-element.8), custom_call_target="InvertDiagBlocksLowerTriangular" | custom-call | tf_op jit(solution)/shard_map/jit(cholesky)/cholesky | solution.py:44
  255.8 0.2 convolution_dynamic-update-slice_fusion.1
  256.0 1.2 convolution_subtract_fusion.2
  257.2 11.7 %cholesky.253 = f32[128,128]{1,0:T(8,128)S(1)} custom-call(f32[128,128]{1,0:T(8,128)S(1)} %convolution_subtract_fusion.2), custom_call_target="Cholesky" | custom-call | tf_op jit(solution)/shard_map/jit(cholesky)/cholesky | solution.py:44
  269.0 0.7 compare_reduce_fusion
  269.7 0.6 compare_reduce_fusion.2
  272.9 0.9 fusion.11
  273.8 2.0 copy.11
  (16 shorter events, 0.2 us)
Async XLA Ops:
  6.5 123.1 %copy-start = (bf16[1,2048,512]{2,1,0:T(8,128)(2,1)S(1)}, bf16[1,2048,512]{2,1,0:T(8,128)(2,1)}, u32[]{:S(2)}) copy-start(bf16[1,2048,512]{2,1,0:T(8,128)(2,1)} %param.7) | copy-start | bytes 6291460
  6.5 171.2 %all-gather.3.cloned.1.call-start = ((), (), s32[]{:S(2)}) async-start(), calls=%async_computation.1 | async-start | bytes 3145728 | tf_op jit(solution)/shard_map/all_gather | solution.py:41
  127.7 1.9 copy-start.1
  184.8 1.0 copy-start.2
Sparse Core Ops, SparseCore 0:
  145.7 32.0 all-gather.2
